TPU v7x, 256 devices: a whole 4x4x8 slice. The times are simulated.
256 devices in a mesh: ctx: 32 (over y, x, core), head: 8 (over z).
Axes of the slice: x: 4, y: 4, z: 8, core: 2. Of those that a mesh axis runs over, the one named last changes fastest.
Arguments:
- queries: bfloat16 [8192, 16384], P(('ctx', 'head')), may hold values from -6 to 6
- keys: bfloat16 [8192, 1024], P(('ctx', 'head')), may hold values from -8 to 8
- values: bfloat16 [8192, 1024], P(('ctx', 'head')), may hold values from -4 to 4
- doc_ids: int32 [8192], replicated, may hold values from 0 to 15, never falling along the last dimension, each value on 1 to 769 neighbouring positions
- grad_out: bfloat16 [8192, 16384], P(('ctx', 'head')), may hold values from -4 to 4
Outputs:
- attn_out: bfloat16 [8192, 16384], P(('ctx', 'head'))
- grad_queries: bfloat16 [8192, 16384], P(('ctx', 'head'))
- grad_keys: bfloat16 [8192, 1024], P(('ctx', 'head'))
- grad_values: bfloat16 [8192, 1024], P(('ctx', 'head'))
Inputs may be any that keep to these rules, and one draw needn't show every extreme that they name: `doc_ids`: document numbers never fall along the sequence; every document holds 1 to 769 tokens and one holds exactly 769.
All inputs are finite; a program needn't handle non-finite values.
Results may differ from a plain program's by a relative error of at most 0.025.
Values may be sent and summed in bfloat16 or wider, within the bound.
A program may use at most 64 MiB of HBM per device.

v0:
```python
import functools
import math

import jax
import jax.numpy as jnp
from jax import lax
from jax.experimental import pallas as pl
from jax.experimental.pallas import tpu as pltpu
from jax.sharding import PartitionSpec as P

HEAD = 128
ROWS = 32
SLOTS = 5
WIN = 800
GROUP_HEADS = 16
SCALE = 1.0 / math.sqrt(HEAD)
LOG2E = math.log2(math.e)
NEG = -1e30


def attend(z, s, qs, dos, k_win, v_win, start):
    f32, bf16 = jnp.float32, jnp.bfloat16
    q_t = qs.T
    do_t = dos.T.astype(f32)
    kk = lax.broadcasted_iota(jnp.int32, (WIN, 128), 0)
    tt = lax.broadcasted_iota(jnp.int32, (WIN, 128), 1) % ROWS
    allowed = (kk >= start) & (kk <= tt + (WIN - ROWS))
    bias = jnp.where(allowed, 0.0, NEG).astype(f32)
    bias = jnp.concatenate([bias] * (GROUP_HEADS * ROWS // 128), axis=1)
    x = jnp.dot(k_win, q_t, preferred_element_type=f32) * (SCALE * LOG2E) + bias
    top = jnp.max(x, axis=0, keepdims=True)
    p = jnp.exp2(x - top)
    total = jnp.sum(p, axis=0, keepdims=True)
    pb = p.astype(bf16)
    inv = 1.0 / total
    out_t = (jnp.dot(v_win.T, pb, preferred_element_type=f32) * inv).astype(bf16)
    delta = jnp.sum(do_t * out_t.astype(f32), axis=0, keepdims=True) * inv
    do_n = (do_t * inv).astype(bf16)
    gp = jnp.dot(v_win, do_n, preferred_element_type=f32)
    gs = (pb.astype(f32) * (gp - delta)).astype(bf16)
    nt = (((1,), (1,)), ((), ()))
    gv = lax.dot_general(pb, do_n, nt, preferred_element_type=f32)
    gk = jnp.dot(gs, qs, preferred_element_type=f32) * SCALE
    gq_t = (jnp.dot(k_win.T, gs, preferred_element_type=f32) * SCALE).astype(bf16)
    return out_t.T, gq_t.T, gk, gv


def stack_heads(x):
    return jnp.concatenate([x[:, h * HEAD:(h + 1) * HEAD] for h in range(GROUP_HEADS)], axis=0)


def spread_heads(ref, x):
    for h in range(GROUP_HEADS):
        ref[0, :, h * HEAD:(h + 1) * HEAD] = x[h * ROWS:(h + 1) * ROWS, :]


def kernel(start_ref, q_ref, do_ref, k_ref, v_ref, o_ref, gq_ref, gk_ref, gv_ref, gk_acc, gv_acc):
    z = lax.axis_index("head")
    s = pl.program_id(1)
    off = pl.multiple_of(s * 256 + z * ROWS, ROWS)
    window = pl.ds(off, WIN)

    @pl.when(s == 0)
    def _():
        gk_acc[...] = jnp.zeros_like(gk_acc)
        gv_acc[...] = jnp.zeros_like(gv_acc)

    out, gq, gk, gv = attend(
        z, s, stack_heads(q_ref[0]), stack_heads(do_ref[0]), k_ref[window, :], v_ref[window, :], start_ref[0]
    )
    spread_heads(o_ref, out)
    spread_heads(gq_ref, gq)
    gk_acc[window, :] += gk
    gv_acc[window, :] += gv

    @pl.when(s == 1)
    def _():
        gk_ref[...] = gk_acc[...].astype(gk_ref.dtype)
        gv_ref[...] = gv_acc[...].astype(gv_ref.dtype)


def compute(starts, q2, do2, k_all, v_all):
    groups = k_all.shape[1] // HEAD
    width = GROUP_HEADS * HEAD
    rows = SLOTS * 256
    tok = pl.BlockSpec((1, ROWS, width), lambda g, s: (s, 0, g))
    key = pl.BlockSpec((rows, HEAD), lambda g, s: (0, g))
    bf16 = jnp.bfloat16
    return pl.pallas_call(
        kernel,
        grid=(groups, 2),
        out_shape=(
            jax.ShapeDtypeStruct(q2.shape, bf16),
            jax.ShapeDtypeStruct(q2.shape, bf16),
            jax.ShapeDtypeStruct(k_all.shape, bf16),
            jax.ShapeDtypeStruct(k_all.shape, bf16),
        ),
        in_specs=[pl.BlockSpec((1, 1, 128), lambda g, s: (s, 0, 0)), tok, tok, key, key],
        out_specs=(tok, tok, key, key),
        scratch_shapes=[pltpu.VMEM((rows, HEAD), jnp.float32)] * 2,
    )(starts, q2, do2, k_all, v_all)


def window_starts(doc_ids, first):
    ids = lax.dynamic_slice_in_dim(doc_ids, first, ROWS)
    begin = jnp.sum((doc_ids[None, :] < ids[:, None]).astype(jnp.int32), axis=1)
    rel = begin - (first - (WIN - ROWS))
    return jnp.tile(rel, 128 // ROWS)[None, :]


def local(queries, keys, values, doc_ids, grad_out):
    c = lax.axis_index("ctx")
    z = lax.axis_index("head")
    n = lax.axis_size("ctx")
    g = c % 2
    pair = c // 2
    swap = [(j, j ^ 1) for j in range(n)]
    ahead = [(j, (j + 2) % n) for j in range(n)]
    back = [(j, (j - 2) % n) for j in range(n)]

    def halves(x):
        half = x.shape[1] // 2
        mine = lax.dynamic_slice_in_dim(x, g * half, half, 1)
        other = lax.dynamic_slice_in_dim(x, (1 - g) * half, half, 1)
        got = lax.ppermute(other, "ctx", swap)
        return jnp.where(g == 0, jnp.stack([mine, got]), jnp.stack([got, mine]))

    def unhalve(x):
        mine = lax.dynamic_index_in_dim(x, g, 0, keepdims=False)
        other = lax.dynamic_index_in_dim(x, 1 - g, 0, keepdims=False)
        got = lax.ppermute(other, "ctx", swap)
        low = jnp.where(g == 0, mine, got)
        high = jnp.where(g == 0, got, mine)
        return jnp.concatenate([low, high], axis=1)

    def gather(x):
        own = halves(x)
        near = lax.ppermute(own, "ctx", ahead)
        far = lax.ppermute(near[1:], "ctx", ahead)
        five = jnp.concatenate([far, near, own], axis=0)
        return lax.all_gather(five, "head", axis=1, tiled=True).reshape(SLOTS * 256, -1)

    def scatter(x):
        five = lax.psum_scatter(x.reshape(SLOTS, 256, -1), "head", scatter_dimension=1, tiled=True).astype(jnp.float32)
        far = lax.ppermute(five[:1], "ctx", back)
        near = jnp.concatenate([five[1:2], five[2:3] + far], axis=0)
        near = lax.ppermute(near, "ctx", back)
        return unhalve(five[3:5] + near).astype(jnp.bfloat16)

    first = pair * 512 + z * ROWS
    starts = jnp.stack([window_starts(doc_ids, first), window_starts(doc_ids, first + 256)])
    q2, do2 = halves(queries), halves(grad_out)
    k_all, v_all = gather(keys), gather(values)
    o2, gq2, gk, gv = compute(starts, q2, do2, k_all, v_all)
    return unhalve(o2), unhalve(gq2), scatter(gk), scatter(gv)


def solution(mesh):
    spec = P(("ctx", "head"), None)
    return jax.shard_map(
        local,
        mesh=mesh,
        in_specs=(spec, spec, spec, P(), spec),
        out_specs=(spec, spec, spec, spec),
        check_vma=False,
    )
```

profile of v0, /device:TPU:1, one launch (start us, length us, event | category | flops | bytes accessed | tf_op | source)
XLA Modules:
  0.0 223.2 jit_solution(5896486491014236932)
XLA Ops:
  7.2 0.8 dynamic-slice_bitcast_fusion.6
  8.0 3.2 %collective-permute-start.5 = (bf16[32,512]{1,0:T(8,128)(2,1)S(1)}, bf16[32,512]{1,0:T(8,128)(2,1)S(1)}, u32[]{:S(2)}, u32[]{:S(2)}) collective-permute-start(bf16[32,512]{1,0:T(8,128)(2,1)S(1)} %get-tuple-element.31), channel_id=1, source_target_pairs={{0,8},{8,0},{16,24},{24,16},{32,40},{40,32},{48,56},{56,48},{64,72... | collective-permute-start | bytes 98312 | tf_op jit(solution)/shard_map/ppermute | solution.py:125
  11.2 0.9 collective-permute-done.5
  12.1 0.1 collective-permute-start.6
  12.2 6.4 %collective-permute-done.6 = bf16[2,32,512]{2,1,0:T(8,128)(2,1)S(1)} collective-permute-done((bf16[2,32,512]{2,1,0:T(8,128)(2,1)S(1)}, bf16[2,32,512]{2,1,0:T(8,128)(2,1)S(1)}, u32[]{:S(2)}, u32[]{:S(2)}) %collective-permute-start.6) | collective-permute-done | bytes 65568 | tf_op jit(solution)/shard_map/ppermute | solution.py:138
  18.6 6.1 %collective-permute-done.7 = bf16[1,32,512]{2,1,0:T(8,128)(2,1)S(1)} collective-permute-done((bf16[1,32,512]{2,1,0:T(8,128)(2,1)S(1)}, bf16[1,32,512]{2,1,0:T(8,128)(2,1)S(1)}, u32[]{:S(2)}, u32[]{:S(2)}) %collective-permute-start.7) | collective-permute-done | bytes 32800 | tf_op jit(solution)/shard_map/ppermute | solution.py:139
  24.7 0.7 pad_maximum_fusion.3
  25.5 0.9 dynamic-slice_bitcast_fusion.7
  26.3 2.6 %collective-permute-start.2 = (bf16[32,512]{1,0:T(8,128)(2,1)S(1)}, bf16[32,512]{1,0:T(8,128)(2,1)S(1)}, u32[]{:S(2)}, u32[]{:S(2)}) collective-permute-start(bf16[32,512]{1,0:T(8,128)(2,1)S(1)} %get-tuple-element.33), channel_id=1, source_target_pairs={{0,8},{8,0},{16,24},{24,16},{32,40},{40,32},{48,56},{56,48},{64,72... | collective-permute-start | bytes 98312 | tf_op jit(solution)/shard_map/ppermute | solution.py:125
  29.0 1.3 dynamic-slice_bitcast_fusion.3
  30.2 0.1 collective-permute-start
  30.4 0.1 collective-permute-start.3
  30.5 0.9 dynamic-slice_bitcast_fusion.2
  31.3 0.5 collective-permute-start.1
  31.8 5.1 %collective-permute-done.3 = bf16[2,32,512]{2,1,0:T(8,128)(2,1)S(1)} collective-permute-done((bf16[2,32,512]{2,1,0:T(8,128)(2,1)S(1)}, bf16[2,32,512]{2,1,0:T(8,128)(2,1)S(1)}, u32[]{:S(2)}, u32[]{:S(2)}) %collective-permute-start.3) | collective-permute-done | bytes 65568 | tf_op jit(solution)/shard_map/ppermute | solution.py:138
  37.0 6.0 %collective-permute-done.4 = bf16[1,32,512]{2,1,0:T(8,128)(2,1)S(1)} collective-permute-done((bf16[1,32,512]{2,1,0:T(8,128)(2,1)S(1)}, bf16[1,32,512]{2,1,0:T(8,128)(2,1)S(1)}, u32[]{:S(2)}, u32[]{:S(2)}) %collective-permute-start.4) | collective-permute-done | bytes 32800 | tf_op jit(solution)/shard_map/ppermute | solution.py:139
  43.0 0.7 pad_maximum_fusion.2
  43.7 0.4 convert_reduce_fusion.1
  44.3 0.1 stack_broadcast_in_dim_tile.6
  44.3 0.6 pad_add_fusion.start_ref
  44.9 1.1 maximum_select_fusion.q_ref
  46.1 1.1 maximum_select_fusion.1.do_ref
  47.2 11.6 %all-gather.5.cloned.1.call-done = bf16[5,256,512]{2,1,0:T(8,128)(2,1)} async-done(((bf16[5,32,512]{2,1,0:T(8,128)(2,1)}), bf16[5,256,512]{2,1,0:T(8,128)(2,1)}) %all-gather.5.cloned.1.call-update) | async-done | bytes 1310736 | tf_op jit(solution)/shard_map/all_gather | solution.py:141
  58.8 38.6 %all-gather.3.cloned.1.call-done = bf16[5,256,512]{2,1,0:T(8,128)(2,1)} async-done(((bf16[5,32,512]{2,1,0:T(8,128)(2,1)}), bf16[5,256,512]{2,1,0:T(8,128)(2,1)}) %all-gather.3.cloned.1.call-update) | async-done | bytes 1310736 | tf_op jit(solution)/shard_map/all_gather | solution.py:141
  97.4 16.3 %shard_map.84 = (bf16[2,32,8192]{2,1,0:T(8,128)(2,1)}, bf16[2,32,8192]{2,1,0:T(8,128)(2,1)}, bf16[1280,512]{1,0:T(8,128)(2,1)}, bf16[1280,512]{1,0:T(8,128)(2,1)}) custom-call(s32[2,1,128]{2,1,0:T(1,128)} %pad_add_fusion.start_ref, bf16[2,32,8192]{2,1,0:T(8,128)(2,1)} %maximum_select_fusion.q_ref, bf16[2,32,8192]{2,1,0:T(8,128)(2,1)} %maximum_select_fusion.1.do_ref, ...), custom_call_target="tpu_custom_call" | custom-call | tf_op jit(solution)/shard_map/pallas_call | solution.py:89
  113.8 1.2 dynamic-slice_bitcast_fusion
  115.0 5.9 %collective-permute-start.9 = (bf16[32,8192]{1,0:T(8,128)(2,1)S(1)}, bf16[32,8192]{1,0:T(8,128)(2,1)}, u32[]{:S(2)}, u32[]{:S(2)}) collective-permute-start(bf16[32,8192]{1,0:T(8,128)(2,1)S(1)} %dynamic-slice_bitcast_fusion), channel_id=1, source_target_pairs={{0,8},{8,0},{16,24},{24,16},{32,40},{40,32},{48,56},{56,48},{64,72... | collective-permute-start | bytes 1572872 | tf_op jit(solution)/shard_map/ppermute | solution.py:131
  120.9 0.1 collective-permute-start.8
  121.0 1.5 collective-permute-done.9
  122.5 1.1 bitcast_select_fusion.1
  123.6 1.1 bitcast_select_fusion.3
  124.8 1.0 pad_maximum_fusion.1
  125.8 1.0 pad_maximum_fusion
  126.8 26.4 %reduce-scatter.5.cloned.1.call-done = bf16[5,32,512]{2,1,0:T(8,128)(2,1)} async-done(((bf16[5,256,512]{2,1,0:T(8,128)(2,1)}), bf16[5,32,512]{2,1,0:T(8,128)(2,1)}) %reduce-scatter.5.cloned.1.call-update) | async-done | bytes 163856 | tf_op jit(solution)/shard_map/reduce_scatter | solution.py:144
  153.3 0.8 fusion.4
  154.0 4.7 %collective-permute-start.13 = (f32[1,32,512]{2,1,0:T(8,128)S(1)}, f32[1,32,512]{2,1,0:T(8,128)S(1)}, u32[]{:S(2)}, u32[]{:S(2)}) collective-permute-start(f32[1,32,512]{2,1,0:T(8,128)S(1)} %get-tuple-element.23), channel_id=1, source_target_pairs={{0,240},{8,248},{16,0},{24,8},{32,16},{40,24},{48,32},{56,40},{64,... | collective-permute-start | bytes 196616 | tf_op jit(solution)/shard_map/ppermute | solution.py:145
  158.7 35.5 %reduce-scatter.3.cloned.1.call-done = bf16[5,32,512]{2,1,0:T(8,128)(2,1)} async-done(((bf16[5,256,512]{2,1,0:T(8,128)(2,1)}), bf16[5,32,512]{2,1,0:T(8,128)(2,1)}) %reduce-scatter.3.cloned.1.call-update) | async-done | bytes 163856 | tf_op jit(solution)/shard_map/reduce_scatter | solution.py:144
  194.2 0.8 fusion.5
  195.0 4.7 %collective-permute-start.10 = (f32[1,32,512]{2,1,0:T(8,128)S(1)}, f32[1,32,512]{2,1,0:T(8,128)S(1)}, u32[]{:S(2)}, u32[]{:S(2)}) collective-permute-start(f32[1,32,512]{2,1,0:T(8,128)S(1)} %get-tuple-element.25), channel_id=1, source_target_pairs={{0,240},{8,248},{16,0},{24,8},{32,16},{40,24},{48,32},{56,40},{64,... | collective-permute-start | bytes 196616 | tf_op jit(solution)/shard_map/ppermute | solution.py:145
  199.7 0.9 convert_element_type.17
  200.6 0.9 convert_element_type.16
  201.6 0.6 collective-permute-start.14
  202.2 4.0 %collective-permute-start.11 = (f32[2,32,512]{2,1,0:T(8,128)S(1)}, f32[2,32,512]{2,1,0:T(8,128)S(1)}, u32[]{:S(2)}, u32[]{:S(2)}) collective-permute-start(f32[2,32,512]{2,1,0:T(8,128)S(1)} %pad_maximum_fusion.4), channel_id=1, source_target_pairs={{0,240},{8,248},{16,0},{24,8},{32,16},{40,24},{48,32},{56,40},{64,... | collective-permute-start | bytes 393224 | tf_op jit(solution)/shard_map/ppermute | solution.py:147
  206.2 6.4 %collective-permute-start.15 = (bf16[32,512]{1,0:T(8,128)(2,1)S(1)}, bf16[32,512]{1,0:T(8,128)(2,1)S(1)}, u32[]{:S(2)}, u32[]{:S(2)}) collective-permute-start(bf16[32,512]{1,0:T(8,128)(2,1)S(1)} %dynamic-slice_bitcast_fusion.4), channel_id=1, source_target_pairs={{0,8},{8,0},{16,24},{24,16},{32,40},{40,32},{48,56},{56,48},{64,72... | collective-permute-start | bytes 98312 | tf_op jit(solution)/shard_map/ppermute | solution.py:131
  212.7 2.5 %collective-permute-start.12 = (bf16[32,512]{1,0:T(8,128)(2,1)S(1)}, bf16[32,512]{1,0:T(8,128)(2,1)S(1)}, u32[]{:S(2)}, u32[]{:S(2)}) collective-permute-start(bf16[32,512]{1,0:T(8,128)(2,1)S(1)} %dynamic-slice_bitcast_fusion.5), channel_id=1, source_target_pairs={{0,8},{8,0},{16,24},{24,16},{32,40},{40,32},{48,56},{56,48},{64,72... | collective-permute-start | bytes 98312 | tf_op jit(solution)/shard_map/ppermute | solution.py:131
  215.2 0.6 pad_maximum_fusion.7
  215.8 0.2 collective-permute-done.12
  216.0 0.6 pad_maximum_fusion.6
  (47 shorter events, 0.6 us)
Async XLA Ops:
  7.2 51.6 %all-gather.5.cloned.1.call-start = ((), (), s32[]{:S(2)}) async-start(), calls=%async_computation.3 | async-start | bytes 1474560 | tf_op jit(solution)/shard_map/all_gather | solution.py:141
  8.0 4.1 %collective-permute-start.5 = (bf16[32,512]{1,0:T(8,128)(2,1)S(1)}, bf16[32,512]{1,0:T(8,128)(2,1)S(1)}, u32[]{:S(2)}, u32[]{:S(2)}) collective-permute-start(bf16[32,512]{1,0:T(8,128)(2,1)S(1)} %get-tuple-element.31), channel_id=1, source_target_pairs={{0,8},{8,0},{16,24},{24,16},{32,40},{40,32},{48,56},{56,48},{64,72... | collective-permute-start | bytes 98312 | tf_op jit(solution)/shard_map/ppermute | solution.py:125
  12.1 6.5 %collective-permute-start.6 = (bf16[2,32,512]{2,1,0:T(8,128)(2,1)S(1)}, bf16[2,32,512]{2,1,0:T(8,128)(2,1)S(1)}, u32[]{:S(2)}, u32[]{:S(2)}) collective-permute-start(bf16[2,32,512]{2,1,0:T(8,128)(2,1)S(1)} %maximum_select_fusion.3), channel_id=1, source_target_pairs={{0,16},{8,24},{16,32},{24,40},{32,48},{40,56},{48,64},{56,72},{64,... | collective-permute-start | bytes 196616 | tf_op jit(solution)/shard_map/ppermute | solution.py:138
  18.6 6.1 %collective-permute-start.7 = (bf16[1,32,512]{2,1,0:T(8,128)(2,1)S(1)}, bf16[1,32,512]{2,1,0:T(8,128)(2,1)S(1)}, u32[]{:S(2)}, u32[]{:S(2)}) collective-permute-start(bf16[1,32,512]{2,1,0:T(8,128)(2,1)S(1)} %slice.41), channel_id=1, source_target_pairs={{0,16},{8,24},{16,32},{24,40},{32,48},{40,56},{48,64},{56,72},{64,... | collective-permute-start | bytes 98312 | tf_op jit(solution)/shard_map/ppermute | solution.py:139
  25.4 5.1 %copy-start = (bf16[32,16384]{1,0:T(8,128)(2,1)S(1)}, bf16[32,16384]{1,0:T(8,128)(2,1)}, u32[]{:S(2)}) copy-start(bf16[32,16384]{1,0:T(8,128)(2,1)} %param.9) | copy-start | bytes 3145732
  25.4 72.0 %all-gather.3.cloned.1.call-start = ((), (), s32[]{:S(2)}) async-start(), calls=%async_computation.2 | async-start | bytes 1474560 | tf_op jit(solution)/shard_map/all_gather | solution.py:141
  26.3 4.0 %collective-permute-start.2 = (bf16[32,512]{1,0:T(8,128)(2,1)S(1)}, bf16[32,512]{1,0:T(8,128)(2,1)S(1)}, u32[]{:S(2)}, u32[]{:S(2)}) collective-permute-start(bf16[32,512]{1,0:T(8,128)(2,1)S(1)} %get-tuple-element.33), channel_id=1, source_target_pairs={{0,8},{8,0},{16,24},{24,16},{32,40},{40,32},{48,56},{56,48},{64,72... | collective-permute-start | bytes 98312 | tf_op jit(solution)/shard_map/ppermute | solution.py:125
  30.2 6.7 %copy-start.3 = (s32[8192]{0:T(1024)S(1)}, s32[8192]{0:T(1024)}, u32[]{:S(2)}) copy-start(s32[8192]{0:T(1024)} %param.8) | copy-start | bytes 98308
  30.2 14.7 %collective-permute-start = (bf16[32,8192]{1,0:T(8,128)(2,1)S(1)}, bf16[32,8192]{1,0:T(8,128)(2,1)S(1)}, u32[]{:S(2)}, u32[]{:S(2)}) collective-permute-start(bf16[32,8192]{1,0:T(8,128)(2,1)S(1)} %get-tuple-element.21), channel_id=1, source_target_pairs={{0,8},{8,0},{16,24},{24,16},{32,40},{40,32},{48,56},{56,48},{64,72... | collective-permute-start | bytes 1572872 | tf_op jit(solution)/shard_map/ppermute | solution.py:125
  30.4 6.5 %collective-permute-start.3 = (bf16[2,32,512]{2,1,0:T(8,128)(2,1)S(1)}, bf16[2,32,512]{2,1,0:T(8,128)(2,1)S(1)}, u32[]{:S(2)}, u32[]{:S(2)}) collective-permute-start(bf16[2,32,512]{2,1,0:T(8,128)(2,1)S(1)} %maximum_select_fusion.2), channel_id=1, source_target_pairs={{0,16},{8,24},{16,32},{24,40},{32,48},{40,56},{48,64},{56,72},{64,... | collective-permute-start | bytes 196616 | tf_op jit(solution)/shard_map/ppermute | solution.py:138
  31.3 14.7 %collective-permute-start.1 = (bf16[32,8192]{1,0:T(8,128)(2,1)}, bf16[32,8192]{1,0:T(8,128)(2,1)S(1)}, u32[]{:S(2)}, u32[]{:S(2)}) collective-permute-start(bf16[32,8192]{1,0:T(8,128)(2,1)} %get-tuple-element.19), channel_id=1, source_target_pairs={{0,8},{8,0},{16,24},{24,16},{32,40},{40,32},{48,56},{56,48},{64,72... | collective-permute-start | bytes 1572872 | tf_op jit(solution)/shard_map/ppermute | solution.py:125
  36.9 6.1 %collective-permute-start.4 = (bf16[1,32,512]{2,1,0:T(8,128)(2,1)S(1)}, bf16[1,32,512]{2,1,0:T(8,128)(2,1)S(1)}, u32[]{:S(2)}, u32[]{:S(2)}) collective-permute-start(bf16[1,32,512]{2,1,0:T(8,128)(2,1)S(1)} %slice.40), channel_id=1, source_target_pairs={{0,16},{8,24},{16,32},{24,40},{32,48},{40,56},{48,64},{56,72},{64,... | collective-permute-start | bytes 98312 | tf_op jit(solution)/shard_map/ppermute | solution.py:139
  43.7 109.6 %reduce-scatter.5.cloned.1.call-start = ((), (), s32[]{:S(2)}) async-start(), calls=%async_computation.5 | async-start | bytes 1474560 | tf_op jit(solution)/shard_map/reduce_scatter | solution.py:144
  113.7 7.1 %copy-start.1 = (bf16[2,32,8192]{2,1,0:T(8,128)(2,1)S(1)}, bf16[2,32,8192]{2,1,0:T(8,128)(2,1)}, u32[]{:S(2)}) copy-start(bf16[2,32,8192]{2,1,0:T(8,128)(2,1)} %get-tuple-element.8) | copy-start | bytes 3145732
  113.8 80.5 %reduce-scatter.3.cloned.1.call-start = ((), (), s32[]{:S(2)}) async-start(), calls=%async_computation.4 | async-start | bytes 1474560 | tf_op jit(solution)/shard_map/reduce_scatter | solution.py:144
  115.0 7.5 %copy-start.2 = (bf16[2,32,8192]{2,1,0:T(8,128)(2,1)S(1)}, bf16[2,32,8192]{2,1,0:T(8,128)(2,1)}, u32[]{:S(2)}) copy-start(bf16[2,32,8192]{2,1,0:T(8,128)(2,1)} %get-tuple-element.9) | copy-start | bytes 3145732
  115.0 7.5 %collective-permute-start.9 = (bf16[32,8192]{1,0:T(8,128)(2,1)S(1)}, bf16[32,8192]{1,0:T(8,128)(2,1)}, u32[]{:S(2)}, u32[]{:S(2)}) collective-permute-start(bf16[32,8192]{1,0:T(8,128)(2,1)S(1)} %dynamic-slice_bitcast_fusion), channel_id=1, source_target_pairs={{0,8},{8,0},{16,24},{24,16},{32,40},{40,32},{48,56},{56,48},{64,72... | collective-permute-start | bytes 1572872 | tf_op jit(solution)/shard_map/ppermute | solution.py:131
  120.9 2.8 %collective-permute-start.8 = (bf16[32,8192]{1,0:T(8,128)(2,1)S(1)}, bf16[32,8192]{1,0:T(8,128)(2,1)}, u32[]{:S(2)}, u32[]{:S(2)}) collective-permute-start(bf16[32,8192]{1,0:T(8,128)(2,1)S(1)} %dynamic-slice_bitcast_fusion.1), channel_id=1, source_target_pairs={{0,8},{8,0},{16,24},{24,16},{32,40},{40,32},{48,56},{56,48},{64,72... | collective-permute-start | bytes 1572872 | tf_op jit(solution)/shard_map/ppermute | solution.py:131
  154.0 47.5 %collective-permute-start.13 = (f32[1,32,512]{2,1,0:T(8,128)S(1)}, f32[1,32,512]{2,1,0:T(8,128)S(1)}, u32[]{:S(2)}, u32[]{:S(2)}) collective-permute-start(f32[1,32,512]{2,1,0:T(8,128)S(1)} %get-tuple-element.23), channel_id=1, source_target_pairs={{0,240},{8,248},{16,0},{24,8},{32,16},{40,24},{48,32},{56,40},{64,... | collective-permute-start | bytes 196616 | tf_op jit(solution)/shard_map/ppermute | solution.py:145
  195.0 7.2 %collective-permute-start.10 = (f32[1,32,512]{2,1,0:T(8,128)S(1)}, f32[1,32,512]{2,1,0:T(8,128)S(1)}, u32[]{:S(2)}, u32[]{:S(2)}) collective-permute-start(f32[1,32,512]{2,1,0:T(8,128)S(1)} %get-tuple-element.25), channel_id=1, source_target_pairs={{0,240},{8,248},{16,0},{24,8},{32,16},{40,24},{48,32},{56,40},{64,... | collective-permute-start | bytes 196616 | tf_op jit(solution)/shard_map/ppermute | solution.py:145
  201.6 4.6 %collective-permute-start.14 = (f32[2,32,512]{2,1,0:T(8,128)S(1)}, f32[2,32,512]{2,1,0:T(8,128)S(1)}, u32[]{:S(2)}, u32[]{:S(2)}) collective-permute-start(f32[2,32,512]{2,1,0:T(8,128)S(1)} %pad_maximum_fusion.5), channel_id=1, source_target_pairs={{0,240},{8,248},{16,0},{24,8},{32,16},{40,24},{48,32},{56,40},{64,... | collective-permute-start | bytes 393224 | tf_op jit(solution)/shard_map/ppermute | solution.py:147
  202.2 10.4 %collective-permute-start.11 = (f32[2,32,512]{2,1,0:T(8,128)S(1)}, f32[2,32,512]{2,1,0:T(8,128)S(1)}, u32[]{:S(2)}, u32[]{:S(2)}) collective-permute-start(f32[2,32,512]{2,1,0:T(8,128)S(1)} %pad_maximum_fusion.4), channel_id=1, source_target_pairs={{0,240},{8,248},{16,0},{24,8},{32,16},{40,24},{48,32},{56,40},{64,... | collective-permute-start | bytes 393224 | tf_op jit(solution)/shard_map/ppermute | solution.py:147
  206.2 8.9 %collective-permute-start.15 = (bf16[32,512]{1,0:T(8,128)(2,1)S(1)}, bf16[32,512]{1,0:T(8,128)(2,1)S(1)}, u32[]{:S(2)}, u32[]{:S(2)}) collective-permute-start(bf16[32,512]{1,0:T(8,128)(2,1)S(1)} %dynamic-slice_bitcast_fusion.4), channel_id=1, source_target_pairs={{0,8},{8,0},{16,24},{24,16},{32,40},{40,32},{48,56},{56,48},{64,72... | collective-permute-start | bytes 98312 | tf_op jit(solution)/shard_map/ppermute | solution.py:131
  212.7 3.3 %collective-permute-start.12 = (bf16[32,512]{1,0:T(8,128)(2,1)S(1)}, bf16[32,512]{1,0:T(8,128)(2,1)S(1)}, u32[]{:S(2)}, u32[]{:S(2)}) collective-permute-start(bf16[32,512]{1,0:T(8,128)(2,1)S(1)} %dynamic-slice_bitcast_fusion.5), channel_id=1, source_target_pairs={{0,8},{8,0},{16,24},{24,16},{32,40},{40,32},{48,56},{56,48},{64,72... | collective-permute-start | bytes 98312 | tf_op jit(solution)/shard_map/ppermute | solution.py:131
Sparse Core Ops, SparseCore 0:
  25.5 33.1 all-gather.4
  60.6 36.7 all-gather.2
  113.9 39.3 reduce-scatter.4
  155.7 38.5 reduce-scatter.2
where the time goes:
time: 224 us; the launch traced here: 223 us
  waiting for transfers between devices  138 us (62%)
  starting transfers between devices  35.5 us (16%)
  Pallas kernels  16.3 us (7%)
  between operations  14 us (6%)
  other arithmetic  12.2 us (5%)
  local copies, waits for them, and re-layouts  6.84 us (3%)
    reduce_scatter x2, waiting for transfers between devices, scatter(): lax.psum_scatter(x.reshape(SLOTS, 256, -1), 'head', scatter_dimension=1,...  61.9 us
    all_gather x2, waiting for transfers between devices, gather(): lax.all_gather(five, 'head', axis=1, tiled=True).reshape(SLOTS * 256, -1)  50.2 us
    pallas_call x1, Pallas kernels, compute(): pl.pallas_call(kernel, grid=(groups, 2), out_shape=(jax.ShapeDtypeStruct(...  16.3 us
    ppermute x4, starting transfers between devices, unhalve(): got = lax.ppermute(other, 'ctx', swap)  14.8 us
    ppermute x2, waiting for transfers between devices, gather(): far = lax.ppermute(near[1:], 'ctx', ahead)  12.1 us
    ppermute x2, waiting for transfers between devices, gather(): near = lax.ppermute(own, 'ctx', ahead)  11.5 us
    ppermute x2, starting transfers between devices, scatter(): far = lax.ppermute(five[:1], 'ctx', back)  9.35 us
    ppermute x4, starting transfers between devices, halves(): got = lax.ppermute(other, 'ctx', swap)  6.44 us
  transfers between devices with their start and end apart: 20, of which 11 were waited for; matrix products, arithmetic and copies ran while one was open for 8% of the time, Pallas kernels for 0%

commit v1 on v0

v1 whole, which is shorter than its diff:
```python
import math

import jax
import jax.numpy as jnp
from jax import lax
from jax.experimental import pallas as pl
from jax.experimental.pallas import tpu as pltpu
from jax.sharding import PartitionSpec as P

HEAD = 128
ROWS = 32
SLOTS = 5
WIN = 800
GROUP_HEADS = 16
GROUPS = 4
KV = 2 * HEAD
RING = 8
HOPS = 4
SCALE = 1.0 / math.sqrt(HEAD)
LOG2E = math.log2(math.e)
NEG = -1e30
MESH = pl.DeviceIdType.MESH
STREAMS = ((3, 4), (1, 2), (0,))


def attend(qs, dos, k_win, v_win, start):
    f32, bf16 = jnp.float32, jnp.bfloat16
    q_t = qs.T
    do_t = dos.T.astype(f32)
    kk = lax.broadcasted_iota(jnp.int32, (WIN, 128), 0)
    tt = lax.broadcasted_iota(jnp.int32, (WIN, 128), 1) % ROWS
    allowed = (kk >= start) & (kk <= tt + (WIN - ROWS))
    bias = jnp.where(allowed, 0.0, NEG).astype(f32)
    bias = jnp.concatenate([bias] * (GROUP_HEADS * ROWS // 128), axis=1)
    x = jnp.dot(k_win, q_t, preferred_element_type=f32) * (SCALE * LOG2E) + bias
    top = jnp.max(x, axis=0, keepdims=True)
    p = jnp.exp2(x - top)
    total = jnp.sum(p, axis=0, keepdims=True)
    pb = p.astype(bf16)
    inv = 1.0 / total
    out_t = (jnp.dot(v_win.T, pb, preferred_element_type=f32) * inv).astype(bf16)
    delta = jnp.sum(do_t * out_t.astype(f32), axis=0, keepdims=True) * inv
    do_n = (do_t * inv).astype(bf16)
    gp = jnp.dot(v_win, do_n, preferred_element_type=f32)
    gs = (pb.astype(f32) * (gp - delta)).astype(bf16)
    nt = (((1,), (1,)), ((), ()))
    gv = lax.dot_general(pb, do_n, nt, preferred_element_type=f32)
    gk = jnp.dot(gs, qs, preferred_element_type=f32) * SCALE
    gq_t = (jnp.dot(k_win.T, gs, preferred_element_type=f32) * SCALE).astype(bf16)
    return out_t.T, gq_t.T, gk, gv


def stack_heads(x):
    return jnp.concatenate([x[:, h * HEAD:(h + 1) * HEAD] for h in range(GROUP_HEADS)], axis=0)


def kernel(
    start_ref, q_hbm, do_hbm, k_hbm, v_hbm,
    o_hbm, gq_hbm, gk_hbm, gv_hbm,
    kv, qd, og, acc, ring_out, ring_in, x_out, x_in, fin,
    kv_loc, kv_send, kv_recv, qd_loc, qd_send, qd_recv,
    gx_send, gx_recv, gz_send, gz_recv,
    rz_send, rz_recv, rx_send, rx_recv,
    o_loc, o_send, o_recv, f_loc, f_send, f_recv,
):
    f32, bf16 = jnp.float32, jnp.bfloat16
    c = lax.axis_index("ctx")
    z = lax.axis_index("head")
    n = lax.axis_size("ctx")
    g = lax.rem(c, 2)
    other = 1 - g
    partner = {"ctx": c + 1 - 2 * g, "head": z}
    ahead = {"ctx": lax.rem(c + 2, n), "head": z}
    behind = {"ctx": lax.rem(c + n - 2, n), "head": z}
    right = {"ctx": c, "head": lax.rem(z + 1, RING)}
    left = {"ctx": c, "head": lax.rem(z + RING - 1, RING)}
    sides = (right, left)
    half = GROUPS * HEAD
    wide = GROUPS * GROUP_HEADS * HEAD

    barrier = pltpu.get_barrier_semaphore()
    for peer in (partner, ahead, behind, right, left):
        pl.semaphore_signal(barrier, inc=1, device_id=peer, device_id_type=MESH)
    pl.semaphore_wait(barrier, 5)

    def remote(src, dst, send, recv, device):
        return pltpu.make_async_remote_copy(
            src_ref=src, dst_ref=dst, send_sem=send, recv_sem=recv, device_id=device, device_id_type=MESH
        )

    def rows(slot, block):
        return pl.ds(pl.multiple_of(slot * (RING * ROWS) + block * ROWS, ROWS), ROWS)

    def cols(group, which):
        return pl.ds(pl.multiple_of(which * half + group * HEAD, HEAD), HEAD)

    drains = []

    local_kv, remote_kv = [], []
    for t, src in enumerate((k_hbm, v_hbm)):
        for j in range(GROUPS):
            dst = kv.at[j, rows(3 + g, z), pl.ds(t * HEAD, HEAD)]
            remote_kv.append(remote(src.at[:, cols(j, other)], dst, kv_send.at[t, j], kv_recv.at[t, j], partner))
            local_kv.append(pltpu.make_async_copy(src.at[:, cols(j, g)], dst, kv_loc.at[t, j]))
    for copy in remote_kv + local_kv:
        copy.start()
    local_qd, remote_qd = [], []
    for t, src in enumerate((q_hbm, do_hbm)):
        mine = src.at[:, pl.ds(pl.multiple_of(g * wide, wide), wide)]
        theirs = src.at[:, pl.ds(pl.multiple_of(other * wide, wide), wide)]
        remote_qd.append(remote(theirs, qd.at[t, g], qd_send.at[t], qd_recv.at[t], partner))
        local_qd.append(pltpu.make_async_copy(mine, qd.at[t, g], qd_loc.at[t]))

    for copy in local_kv:
        copy.wait()
    for t, src in enumerate((k_hbm, v_hbm)):
        for j in range(GROUPS):
            dst = kv.at[j, rows(3 + other, z), pl.ds(t * HEAD, HEAD)]
            remote(src.at[:, cols(j, g)], dst, kv_send.at[t, j], kv_recv.at[t, j], partner).wait_recv()
    drains += remote_kv

    def block_of(direction, distance):
        if direction == 0:
            return lax.rem(z + RING - distance, RING)
        return lax.rem(z + distance, RING)

    def lanes(direction, hop):
        if hop < HOPS:
            return pl.ds(0, KV)
        return pl.ds(direction * HEAD, HEAD)

    def gather_copy(slot, direction, hop, distance):
        block = kv.at[:, rows(slot, block_of(direction, distance)), lanes(direction, hop)]
        return remote(
            block, block, gz_send.at[slot, direction, hop - 1], gz_recv.at[slot, direction, hop - 1], sides[direction]
        )

    def shift_copy(index, source, target):
        return remote(
            kv.at[:, rows(source, z), :], kv.at[:, rows(target, z), :], gx_send.at[index], gx_recv.at[index], ahead
        )

    shifts = [shift_copy(0, 3, 1), shift_copy(1, 4, 2), shift_copy(2, 2, 0)]
    shift_in = {1: shifts[0], 2: shifts[1], 0: shifts[2]}

    for step in range(1, HOPS + 4):
        for first, stream in enumerate(STREAMS):
            hop = step - first
            if hop < 1 or hop > HOPS + 1:
                continue
            for slot in stream:
                if hop == 1:
                    if slot < 3:
                        shift_in[slot].wait_recv()
                    if slot == 2:
                        shifts[2].start()
                        drains.append(shifts[2])
                else:
                    for direction in range(2):
                        gather_copy(slot, direction, hop - 1, hop - 1).wait_recv()
                if hop <= HOPS:
                    for direction in range(2):
                        copy = gather_copy(slot, direction, hop, hop - 1)
                        copy.start()
                        drains.append(copy)
            if step == 1 and first == 0:
                for copy in shifts[:2]:
                    copy.start()
                    drains.append(copy)
                for copy in remote_qd + local_qd:
                    copy.start()
                acc[...] = jnp.zeros_like(acc)

    for t, src in enumerate((q_hbm, do_hbm)):
        local_qd[t].wait()
        mine = src.at[:, pl.ds(pl.multiple_of(g * wide, wide), wide)]
        remote(mine, qd.at[t, other], qd_send.at[t], qd_recv.at[t], partner).wait_recv()
    drains += remote_qd

    def compute(index, carry):
        j = index // 2
        s = index % 2
        window = pl.ds(pl.multiple_of(s * (RING * ROWS) + z * ROWS, ROWS), WIN)
        heads = pl.ds(pl.multiple_of(j * (GROUP_HEADS * HEAD), GROUP_HEADS * HEAD), GROUP_HEADS * HEAD)
        out, gq, gk, gv = attend(
            stack_heads(qd[0, s, :, heads]), stack_heads(qd[1, s, :, heads]),
            kv[j, window, pl.ds(0, HEAD)], kv[j, window, pl.ds(HEAD, HEAD)], start_ref[s],
        )
        for h in range(GROUP_HEADS):
            at = pl.ds(pl.multiple_of(j * (GROUP_HEADS * HEAD) + h * HEAD, HEAD), HEAD)
            og[0, s, :, at] = out[h * ROWS:(h + 1) * ROWS, :]
            og[1, s, :, at] = gq[h * ROWS:(h + 1) * ROWS, :]
        acc[j, window, pl.ds(0, HEAD)] += gk
        acc[j, window, pl.ds(HEAD, HEAD)] += gv
        return carry

    lax.fori_loop(0, 2 * GROUPS, compute, 0)

    own_out = []
    for t, dst in enumerate((o_hbm, gq_hbm)):
        place = dst.at[:, pl.ds(pl.multiple_of(g * wide, wide), wide)]
        copy = remote(og.at[t, other], place, o_send.at[t], o_recv.at[t], partner)
        copy.start()
        drains.append(copy)
        copy = pltpu.make_async_copy(og.at[t, g], place, o_loc.at[t])
        copy.start()
        own_out.append(copy)

    def reduce_copy(slot, direction, hop):
        part = lanes(direction, HOPS + 1 - hop)
        at = (direction, hop - 1, slot)
        return remote(
            ring_out.at[at + (slice(None), slice(None), part)], ring_in.at[at + (slice(None), slice(None), part)],
            rz_send.at[at], rz_recv.at[at], sides[direction],
        )

    def x_copy(slot):
        return remote(x_out.at[slot], x_in.at[slot], rx_send.at[slot], rx_recv.at[slot], behind)

    def own_total(slot):
        total = acc[:, rows(slot, z), :]
        return total + (ring_in[0, HOPS - 1, slot].astype(f32) + ring_in[1, HOPS - 1, slot].astype(f32))

    for step in range(1, HOPS + 4):
        for first, stream in enumerate(reversed(STREAMS)):
            hop = step - first
            if hop < 1 or hop > HOPS + 1:
                continue
            for slot in stream:
                if hop > 1:
                    for direction in range(2):
                        reduce_copy(slot, direction, hop - 1).wait_recv()
                if hop <= HOPS:
                    for direction in range(2):
                        part = lanes(direction, HOPS + 1 - hop)
                        block = rows(slot, block_of(1 - direction, HOPS + 1 - hop))
                        value = acc[:, block, part]
                        if hop == 2:
                            low = ring_in[direction, 0, slot, :, :, pl.ds(direction * HEAD, HEAD)].astype(f32)
                            here = pl.ds(direction * HEAD, HEAD)
                            away = pl.ds((1 - direction) * HEAD, HEAD)
                            ring_out[direction, 1, slot, :, :, here] = (acc[:, block, here] + low).astype(bf16)
                            ring_out[direction, 1, slot, :, :, away] = acc[:, block, away].astype(bf16)
                        else:
                            if hop > 2:
                                value = value + ring_in[direction, hop - 2, slot].astype(f32)
                            ring_out[direction, hop - 1, slot, :, :, part] = value.astype(bf16)
                        copy = reduce_copy(slot, direction, hop)
                        copy.start()
                        drains.append(copy)
                elif slot < 3:
                    total = own_total(slot)
                    if slot == 2:
                        x_copy(0).wait_recv()
                        total = total + x_in[0].astype(f32)
                    x_out[slot] = total.astype(bf16)
                    copy = x_copy(slot)
                    copy.start()
                    drains.append(copy)
                else:
                    total = own_total(slot)
                    x_copy(slot - 2).wait_recv()
                    fin[slot - 3] = (total + x_in[slot - 2].astype(f32)).astype(bf16)

    own_fin = []
    for t, dst in enumerate((gk_hbm, gv_hbm)):
        for j in range(GROUPS):
            place = dst.at[:, cols(j, g)]
            part = pl.ds(t * HEAD, HEAD)
            copy = remote(fin.at[other, j, :, part], place, f_send.at[t, j], f_recv.at[t, j], partner)
            copy.start()
            drains.append(copy)
            copy = pltpu.make_async_copy(fin.at[g, j, :, part], place, f_loc.at[t, j])
            copy.start()
            own_fin.append(copy)

    for copy in own_out + own_fin:
        copy.wait()
    for t, dst in enumerate((o_hbm, gq_hbm)):
        place = dst.at[:, pl.ds(pl.multiple_of(other * wide, wide), wide)]
        remote(og.at[t, g], place, o_send.at[t], o_recv.at[t], partner).wait_recv()
    for t, dst in enumerate((gk_hbm, gv_hbm)):
        for j in range(GROUPS):
            place = dst.at[:, cols(j, other)]
            remote(fin.at[g, j, :, pl.ds(t * HEAD, HEAD)], place, f_send.at[t, j], f_recv.at[t, j], partner).wait_recv()
    for copy in drains:
        copy.wait_send()


def attention(starts, queries, grad_out, keys, values):
    bf16 = jnp.bfloat16
    dma = pltpu.SemaphoreType.DMA
    any_space = pl.BlockSpec(memory_space=pl.ANY)
    wide = GROUPS * GROUP_HEADS * HEAD
    return pl.pallas_call(
        kernel,
        out_shape=(
            jax.ShapeDtypeStruct(queries.shape, bf16),
            jax.ShapeDtypeStruct(queries.shape, bf16),
            jax.ShapeDtypeStruct(keys.shape, bf16),
            jax.ShapeDtypeStruct(keys.shape, bf16),
        ),
        in_specs=[pl.BlockSpec(memory_space=pltpu.VMEM)] + [any_space] * 4,
        out_specs=(any_space,) * 4,
        scratch_shapes=[
            pltpu.VMEM((GROUPS, SLOTS * RING * ROWS, KV), bf16),
            pltpu.VMEM((2, 2, ROWS, wide), bf16),
            pltpu.VMEM((2, 2, ROWS, wide), bf16),
            pltpu.VMEM((GROUPS, SLOTS * RING * ROWS, KV), jnp.float32),
            pltpu.VMEM((2, HOPS, SLOTS, GROUPS, ROWS, KV), bf16),
            pltpu.VMEM((2, HOPS, SLOTS, GROUPS, ROWS, KV), bf16),
            pltpu.VMEM((3, GROUPS, ROWS, KV), bf16),
            pltpu.VMEM((3, GROUPS, ROWS, KV), bf16),
            pltpu.VMEM((2, GROUPS, ROWS, KV), bf16),
            dma((2, GROUPS)), dma((2, GROUPS)), dma((2, GROUPS)),
            dma((2,)), dma((2,)), dma((2,)),
            dma((3,)), dma((3,)),
            dma((SLOTS, 2, HOPS)), dma((SLOTS, 2, HOPS)),
            dma((2, HOPS, SLOTS)), dma((2, HOPS, SLOTS)),
            dma((3,)), dma((3,)),
            dma((2,)), dma((2,)), dma((2,)),
            dma((2, GROUPS)), dma((2, GROUPS)), dma((2, GROUPS)),
        ],
        compiler_params=pltpu.CompilerParams(
            collective_id=0, has_side_effects=True, vmem_limit_bytes=56 * 1024 * 1024
        ),
    )(starts, queries, grad_out, keys, values)


def window_starts(doc_ids, first):
    ids = lax.dynamic_slice_in_dim(doc_ids, first, ROWS)
    begin = jnp.sum((doc_ids[None, :] < ids[:, None]).astype(jnp.int32), axis=1)
    rel = begin - (first - (WIN - ROWS))
    return jnp.tile(rel, 128 // ROWS)[None, :]


def local(queries, keys, values, doc_ids, grad_out):
    first = lax.axis_index("ctx") // 2 * (2 * RING * ROWS) + lax.axis_index("head") * ROWS
    starts = jnp.stack([window_starts(doc_ids, first), window_starts(doc_ids, first + RING * ROWS)])
    return attention(starts, queries, grad_out, keys, values)


def solution(mesh):
    spec = P(("ctx", "head"), None)
    return jax.shard_map(
        local,
        mesh=mesh,
        in_specs=(spec, spec, spec, P(), spec),
        out_specs=(spec, spec, spec, spec),
        check_vma=False,
    )
```

time: 224 us -> 100 us (0.45)
  waiting for transfers between devices: 138 us -> 0 us
  Pallas kernels: 16.3 us -> 92.6 us
  starting transfers between devices: 35.5 us -> 0 us
  between operations: 14 us -> 0.7 us
  other arithmetic: 12.2 us -> 0.99 us
    pallas_call x1, Pallas kernels: 16.3 us -> 92.6 us  [attention(): pl.pallas_call(kernel, out_shape=(jax.ShapeDtypeStruct(queries.shape, bf1...]
    reduce_scatter x2 -> x0, waiting for transfers between devices: 61.9 us -> none  [scatter(): lax.psum_scatter(x.reshape(SLOTS, 256, -1), 'head', scatter_dimension=1,...]
    all_gather x2 -> x0, waiting for transfers between devices: 50.2 us -> none  [gather(): lax.all_gather(five, 'head', axis=1, tiled=True).reshape(SLOTS * 256, -1)]
    ppermute x16 -> x0, starting transfers between devices: 35.3 us -> none  [the longest x4 14.8 us: unhalve(): got = lax.ppermute(other, 'ctx', swap)]
    ppermute x16 -> x0, waiting for transfers between devices: 26.1 us -> none  [the longest x2 12.1 us: gather(): far = lax.ppermute(near[1:], 'ctx', ahead)]
    unnamed x8 -> x12, local copies, waits for them, and re-layouts: 0.02 us -> 5.55 us
    concatenate x8 -> x0, other arithmetic: 4.74 us -> none  [the longest x4 3.35 us: unhalve(): return jnp.concatenate([low, high], axis=1)]
    select_n x6 -> x0, other arithmetic: 4.52 us -> none  [the longest x4 2.28 us: halves(): return jnp.where(g == 0, jnp.stack([mine, got]), jnp.stack([got, mine]))]
  transfers between devices with their start and end apart: 20 -> 0, of which waited for: 11 -> 0; matrix products, arithmetic and copies ran while one was open for 8% -> 0% of each run, Pallas kernels for 0% -> 0%
where the time goes in v1:
time: 100 us
  Pallas kernels  92.6 us (93%)
  local copies, waits for them, and re-layouts  5.79 us (6%)
    pallas_call x1, Pallas kernels, attention(): pl.pallas_call(kernel, out_shape=(jax.ShapeDtypeStruct(queries.shape, bf1...  92.6 us
    unnamed x12, local copies, waits for them, and re-layouts  5.55 us

profile of v1, /device:TPU:1, one launch (start us, length us, event | category | flops | bytes accessed | tf_op | source)
XLA Modules:
  0.0 100.1 jit_solution(7458894835126246636)
XLA Ops:
  0.6 0.0 copy-start.3
  0.7 0.7 copy-done.3
  1.4 0.1 fusion
  1.5 0.4 convert_reduce_fusion.1
  1.9 0.1 stack_broadcast_in_dim_tile.7
  2.0 0.1 stack_broadcast_in_dim_tile.6
  2.1 0.6 pad_add_fusion.start_ref
  2.6 92.6 %shard_map.84 = (bf16[32,16384]{1,0:T(8,128)(2,1)}, bf16[32,16384]{1,0:T(8,128)(2,1)}, bf16[32,1024]{1,0:T(8,128)(2,1)}, bf16[32,1024]{1,0:T(8,128)(2,1)}) custom-call(s32[2,1,128]{2,1,0:T(1,128)} %pad_add_fusion.start_ref, bf16[32,16384]{1,0:T(8,128)(2,1)} %q_hbm.1, bf16[32,16384]{1,0:T(8,128)(2,1)} %do_hbm.1, bf16[32,1024]{1,0:T(8,128)(2,1)} %k_hbm.1, ...), custom_call_target="tpu_custom_call" | custom-call | tf_op jit(solution)/shard_map/pallas_call | solution.py:295
  95.2 0.0 copy-start
  95.3 2.4 %copy.13 = bf16[32,16384]{1,0:T(8,128)(2,1)} copy(bf16[32,16384]{1,0:T(8,128)(2,1)} %get-tuple-element.14) | data formatting | bytes 2097152
  97.6 0.0 copy-done
  97.6 0.0 copy-start.2
  97.6 1.0 copy.14
  98.6 0.0 copy-done.2
  98.6 0.0 copy-start.1
  98.6 0.6 copy.15
  99.2 0.2 copy-done.1
  99.4 0.6 copy.16
  (3 shorter events, 0.0 us)
Async XLA Ops:
  0.6 0.8 copy-start.3
  95.2 2.4 %copy-start = (bf16[32,16384]{1,0:T(8,128)(2,1)S(1)}, bf16[32,16384]{1,0:T(8,128)(2,1)}, u32[]{:S(2)}) copy-start(bf16[32,16384]{1,0:T(8,128)(2,1)} %get-tuple-element.15) | copy-start | bytes 3145732
  97.6 1.0 copy-start.2
  98.6 0.9 copy-start.1

commit v2 on v1

v2 whole, which is shorter than its diff:
```python
import math

import jax
import jax.numpy as jnp
from jax import lax
from jax.experimental import pallas as pl
from jax.experimental.pallas import tpu as pltpu
from jax.sharding import PartitionSpec as P

HEAD = 128
ROWS = 32
SLOTS = 5
WIN = 800
GROUP_HEADS = 16
GROUPS = 4
KV = 2 * HEAD
RING = 8
HOPS = 4
SCALE = 1.0 / math.sqrt(HEAD)
LOG2E = math.log2(math.e)
NEG = -1e30
MESH = pl.DeviceIdType.MESH
SHIFT = {1: 3, 2: 4, 0: 4}
SPOTS = ((0,), (1, -1), (2, -2), (3, -3), (4,))
ORDER = (4, 3, -3, 2, -2, 1, -1, 0)
CHUNK = 2


def attend(qs, dos, k_win, v_win, start):
    f32, bf16 = jnp.float32, jnp.bfloat16
    q_t = qs.T
    do_t = dos.T.astype(f32)
    kk = lax.broadcasted_iota(jnp.int32, (WIN, 128), 0)
    tt = lax.broadcasted_iota(jnp.int32, (WIN, 128), 1) % ROWS
    allowed = (kk >= start) & (kk <= tt + (WIN - ROWS))
    bias = jnp.where(allowed, 0.0, NEG).astype(f32)
    bias = jnp.concatenate([bias] * (GROUP_HEADS * ROWS // 128), axis=1)
    x = jnp.dot(k_win, q_t, preferred_element_type=f32) * (SCALE * LOG2E) + bias
    top = jnp.max(x, axis=0, keepdims=True)
    p = jnp.exp2(x - top)
    total = jnp.sum(p, axis=0, keepdims=True)
    pb = p.astype(bf16)
    inv = 1.0 / total
    out_t = (jnp.dot(v_win.T, pb, preferred_element_type=f32) * inv).astype(bf16)
    delta = jnp.sum(do_t * out_t.astype(f32), axis=0, keepdims=True) * inv
    do_n = (do_t * inv).astype(bf16)
    gp = jnp.dot(v_win, do_n, preferred_element_type=f32)
    gs = (pb.astype(f32) * (gp - delta)).astype(bf16)
    nt = (((1,), (1,)), ((), ()))
    gv = lax.dot_general(pb, do_n, nt, preferred_element_type=f32)
    gk = jnp.dot(gs, qs, preferred_element_type=f32) * SCALE
    gq_t = (jnp.dot(k_win.T, gs, preferred_element_type=f32) * SCALE).astype(bf16)
    return out_t.T, gq_t.T, gk, gv


def stack_heads(x):
    return jnp.concatenate([x[:, h * HEAD:(h + 1) * HEAD] for h in range(GROUP_HEADS)], axis=0)


def kernel(
    start_ref, q_hbm, do_hbm, k_hbm, v_hbm,
    o_hbm, gq_hbm, gk_hbm, gv_hbm,
    kv, qd, og, acc, ring_out, ring_in, x_out, x_in, fin,
    kv_loc, kv_send, kv_recv, qd_loc, qd_send, qd_recv,
    gx_send, gx_recv, gz_send, gz_recv,
    rz_send, rz_recv, rx_send, rx_recv,
    o_loc, o_send, o_recv, f_loc, f_send, f_recv,
):
    f32, bf16 = jnp.float32, jnp.bfloat16
    c = lax.axis_index("ctx")
    z = lax.axis_index("head")
    n = lax.axis_size("ctx")
    g = lax.rem(c, 2)
    other = 1 - g
    partner = {"ctx": c + 1 - 2 * g, "head": z}
    ahead = {"ctx": lax.rem(c + 2, n), "head": z}
    behind = {"ctx": lax.rem(c + n - 2, n), "head": z}
    ahead2 = {"ctx": lax.rem(c + 4, n), "head": z}
    behind2 = {"ctx": lax.rem(c + n - 4, n), "head": z}
    right = {"ctx": c, "head": lax.rem(z + 1, RING)}
    left = {"ctx": c, "head": lax.rem(z + RING - 1, RING)}
    sides = (right, left)
    half = GROUPS * HEAD
    wide = GROUPS * GROUP_HEADS * HEAD

    barrier = pltpu.get_barrier_semaphore()
    for peer in (partner, ahead, behind, ahead2, behind2, right, left):
        pl.semaphore_signal(barrier, inc=1, device_id=peer, device_id_type=MESH)
    pl.semaphore_wait(barrier, 7)

    def remote(src, dst, send, recv, device):
        return pltpu.make_async_remote_copy(
            src_ref=src, dst_ref=dst, send_sem=send, recv_sem=recv, device_id=device, device_id_type=MESH
        )

    def rows(slot, block):
        return pl.ds(pl.multiple_of(slot * (RING * ROWS) + block * ROWS, ROWS), ROWS)

    def cols(group, which):
        return pl.ds(pl.multiple_of(which * half + group * HEAD, HEAD), HEAD)

    def near(distance):
        return lax.rem(z + distance % RING, RING)

    def members(chunk):
        return pl.ds(chunk * CHUNK, CHUNK)

    drains = []

    def launch(copy):
        copy.start()
        drains.append(copy)

    local_kv, remote_kv = [], []
    for j in range(GROUPS):
        for t, src in enumerate((k_hbm, v_hbm)):
            dst = kv.at[j, rows(3 + g, z), pl.ds(t * HEAD, HEAD)]
            remote_kv.append(remote(src.at[:, cols(j, other)], dst, kv_send.at[t, j], kv_recv.at[t, j], partner))
            local_kv.append(pltpu.make_async_copy(src.at[:, cols(j, g)], dst, kv_loc.at[t, j]))
    for copy in remote_kv:
        launch(copy)
    for copy in local_kv:
        copy.start()
    local_qd, remote_qd = [], []
    for t, src in enumerate((q_hbm, do_hbm)):
        mine = src.at[:, pl.ds(pl.multiple_of(g * wide, wide), wide)]
        theirs = src.at[:, pl.ds(pl.multiple_of(other * wide, wide), wide)]
        remote_qd.append(remote(theirs, qd.at[t, g], qd_send.at[t], qd_recv.at[t], partner))
        local_qd.append(pltpu.make_async_copy(mine, qd.at[t, g], qd_loc.at[t]))
    for copy in local_kv:
        copy.wait()

    def await_own(chunk):
        for t, src in enumerate((k_hbm, v_hbm)):
            for j in range(chunk * CHUNK, (chunk + 1) * CHUNK):
                dst = kv.at[j, rows(3 + other, z), pl.ds(t * HEAD, HEAD)]
                remote(src.at[:, cols(j, g)], dst, kv_send.at[t, j], kv_recv.at[t, j], partner).wait_recv()

    def lanes(direction, hop):
        if hop < HOPS:
            return pl.ds(0, KV)
        return pl.ds(direction * HEAD, HEAD)

    def gather_copy(chunk, slot, direction, hop, distance):
        block = kv.at[members(chunk), rows(slot, near(distance)), lanes(direction, hop)]
        at = (chunk, slot, direction, hop - 1)
        return remote(block, block, gz_send.at[at], gz_recv.at[at], sides[direction])

    def gather_wait(chunk, slot, hop):
        for direction, sign in enumerate((-1, 1)):
            gather_copy(chunk, slot, direction, hop, sign * hop).wait_recv()

    def gather_hop(chunk, slot, hop):
        for direction, sign in enumerate((-1, 1)):
            launch(gather_copy(chunk, slot, direction, hop, sign * (hop - 1)))

    def shift_copy(chunk, target, distance):
        source = SHIFT[target]
        at = (chunk, target, distance % RING)
        block = near(distance)
        return remote(
            kv.at[members(chunk), rows(source, block), :], kv.at[members(chunk), rows(target, block), :],
            gx_send.at[at], gx_recv.at[at], ahead if target else ahead2,
        )

    def gather_far(chunk, step):
        if step == 0:
            launch(shift_copy(chunk, 0, 0))
        elif step == 1:
            shift_copy(chunk, 0, 0).wait_recv()
        else:
            gather_wait(chunk, 0, step - 1)
        if 1 <= step <= HOPS:
            gather_hop(chunk, 0, step)

    def gather_x_first(chunk):
        for step in range(HOPS + 2):
            for slot in (4, 3):
                if 1 <= step <= HOPS:
                    gather_wait(chunk, slot, step)
                if step < HOPS:
                    gather_hop(chunk, slot, step + 1)
                if step == 0:
                    launch(shift_copy(chunk, slot - 2, 0))
            for slot in (2, 1):
                if step == 1:
                    shift_copy(chunk, slot, 0).wait_recv()
                elif step > 1:
                    gather_wait(chunk, slot, step - 1)
                if 1 <= step <= HOPS:
                    gather_hop(chunk, slot, step)
            gather_far(chunk, step)
            yield

    def gather_z_first(chunk):
        for step in range(HOPS + 2):
            if step <= HOPS:
                for slot in (4, 3):
                    if step > 0:
                        gather_wait(chunk, slot, step)
                    if step < HOPS:
                        gather_hop(chunk, slot, step + 1)
                    for distance in SPOTS[step]:
                        launch(shift_copy(chunk, slot - 2, distance))
            gather_far(chunk, step)
            if step > HOPS:
                for spot in SPOTS:
                    for distance in spot:
                        for slot in (2, 1):
                            shift_copy(chunk, slot, distance).wait_recv()
            yield

    def attend_rows(j, s):
        window = pl.ds(pl.multiple_of(s * (RING * ROWS) + z * ROWS, ROWS), WIN)
        heads = pl.ds(pl.multiple_of(j * (GROUP_HEADS * HEAD), GROUP_HEADS * HEAD), GROUP_HEADS * HEAD)
        out, gq, gk, gv = attend(
            stack_heads(qd[0, s, :, heads]), stack_heads(qd[1, s, :, heads]),
            kv[j, window, pl.ds(0, HEAD)], kv[j, window, pl.ds(HEAD, HEAD)], start_ref[s],
        )
        for h in range(GROUP_HEADS):
            at = pl.ds(pl.multiple_of(j * (GROUP_HEADS * HEAD) + h * HEAD, HEAD), HEAD)
            og[0, s, :, at] = out[h * ROWS:(h + 1) * ROWS, :]
            og[1, s, :, at] = gq[h * ROWS:(h + 1) * ROWS, :]
        acc[j, window, pl.ds(0, HEAD)] += gk
        acc[j, window, pl.ds(HEAD, HEAD)] += gv

    def reduce_copy(j, slot, direction, hop):
        part = lanes(direction, HOPS + 1 - hop)
        at = (j, direction, hop - 1, slot)
        view = at + (slice(None), part)
        return remote(ring_out.at[view], ring_in.at[view], rz_send.at[at], rz_recv.at[at], sides[direction])

    def reduce_wait(j, slot, hop):
        for direction in range(2):
            reduce_copy(j, slot, direction, hop).wait_recv()

    def reduce_hop(j, slot, hop):
        for direction, sign in enumerate((1, -1)):
            block = rows(slot, near(sign * (HOPS + 1 - hop)))
            out = (j, direction, hop - 1, slot, slice(None))
            came = (j, direction, hop - 2, slot, slice(None))
            if hop == 2:
                here = pl.ds(direction * HEAD, HEAD)
                away = pl.ds((1 - direction) * HEAD, HEAD)
                ring_out[out + (here,)] = (acc[j, block, here] + ring_in[came + (here,)].astype(f32)).astype(bf16)
                ring_out[out + (away,)] = acc[j, block, away].astype(bf16)
            else:
                part = lanes(direction, HOPS + 1 - hop)
                value = acc[j, block, part]
                if hop > 2:
                    value = value + ring_in[came + (part,)].astype(f32)
                ring_out[out + (part,)] = value.astype(bf16)
            launch(reduce_copy(j, slot, direction, hop))

    def ring_total(j, slot):
        total = acc[j, rows(slot, z), :]
        return total + (ring_in[j, 0, HOPS - 1, slot].astype(f32) + ring_in[j, 1, HOPS - 1, slot].astype(f32))

    def x_copy(j, slot, distance):
        at = (j, slot, distance % RING)
        device = behind if slot else behind2
        return remote(x_out.at[at], x_in.at[at], rx_send.at[at], rx_recv.at[at], device)

    def send_total(j, slot):
        x_out[j, slot, 0] = ring_total(j, slot).astype(bf16)
        launch(x_copy(j, slot, 0))

    def ring_step(j, slot, step):
        if step > 0:
            reduce_wait(j, slot, step)
        if step < HOPS:
            reduce_hop(j, slot, step + 1)

    def reduce_z_first(j):
        for step in range(HOPS + 2):
            if step <= HOPS:
                for slot in (0, 2, 1):
                    ring_step(j, slot, step)
                    if step == HOPS:
                        send_total(j, slot)
                for slot in (4, 3):
                    ring_step(j, slot, step)
            else:
                for slot in (4, 3):
                    total = ring_total(j, slot)
                    x_copy(j, slot - 2, 0).wait_recv()
                    total = total + x_in[j, slot - 2, 0].astype(f32)
                    if slot == 4:
                        x_copy(j, 0, 0).wait_recv()
                        total = total + x_in[j, 0, 0].astype(f32)
                    fin[slot - 3, j] = total.astype(bf16)
            yield

    def reduce_x_first(j):
        for step in range(HOPS + 2):
            if step > 0:
                for slot in (4, 3):
                    for distance in SPOTS[HOPS + 1 - step]:
                        x_copy(j, slot - 2, distance).wait_recv()
                        place = rows(slot, near(distance))
                        acc[j, place, :] = acc[j, place, :] + x_in[j, slot - 2, distance % RING].astype(f32)
                    ring_step(j, slot, step - 1)
            if step <= HOPS:
                ring_step(j, 0, step)
                if step == HOPS:
                    send_total(j, 0)
            if step == 0:
                for distance in ORDER:
                    for slot in (2, 1):
                        x_out[j, slot, distance % RING] = acc[j, rows(slot, near(distance)), :].astype(bf16)
                        launch(x_copy(j, slot, distance))
            if step > HOPS:
                fin[0, j] = ring_total(j, 3).astype(bf16)
                total = ring_total(j, 4)
                x_copy(j, 0, 0).wait_recv()
                fin[1, j] = (total + x_in[j, 0, 0].astype(f32)).astype(bf16)
            yield

    own_fin = []

    def finish(j):
        for t, dst in enumerate((gk_hbm, gv_hbm)):
            place = dst.at[:, cols(j, g)]
            part = pl.ds(t * HEAD, HEAD)
            launch(remote(fin.at[other, j, :, part], place, f_send.at[t, j], f_recv.at[t, j], partner))
            copy = pltpu.make_async_copy(fin.at[g, j, :, part], place, f_loc.at[t, j])
            copy.start()
            own_fin.append(copy)

    z_first, x_first = gather_z_first(0), gather_x_first(1)
    await_own(0)
    next(z_first)
    await_own(1)
    next(x_first)
    for copy in remote_qd:
        launch(copy)
    for copy in local_qd:
        copy.start()
    acc[...] = jnp.zeros_like(acc)
    next(z_first)
    for step in range(HOPS):
        next(z_first)
        if step < HOPS - 1:
            next(x_first)

    for t, src in enumerate((q_hbm, do_hbm)):
        local_qd[t].wait()
        mine = src.at[:, pl.ds(pl.multiple_of(g * wide, wide), wide)]
        remote(mine, qd.at[t, other], qd_send.at[t], qd_recv.at[t], partner).wait_recv()

    backs = []
    for j in range(GROUPS):
        if j == 0:
            for s in range(2):
                attend_rows(j, s)
                next(x_first)
        else:
            lax.fori_loop(0, 2, lambda s, carry, j=j: (attend_rows(j, s), carry)[1], 0)
        backs.insert(0, reduce_z_first(j) if j < CHUNK else reduce_x_first(j))
        for back in backs:
            next(back)

    own_out = []
    for t, dst in enumerate((o_hbm, gq_hbm)):
        place = dst.at[:, pl.ds(pl.multiple_of(g * wide, wide), wide)]
        launch(remote(og.at[t, other], place, o_send.at[t], o_recv.at[t], partner))
        copy = pltpu.make_async_copy(og.at[t, g], place, o_loc.at[t])
        copy.start()
        own_out.append(copy)

    for step in range(1, HOPS + 2):
        for index, back in enumerate(backs):
            if step + index < HOPS + 2:
                next(back)
                if step + index == HOPS + 1:
                    finish(GROUPS - 1 - index)

    for copy in own_out + own_fin:
        copy.wait()
    for t, dst in enumerate((o_hbm, gq_hbm)):
        place = dst.at[:, pl.ds(pl.multiple_of(other * wide, wide), wide)]
        remote(og.at[t, g], place, o_send.at[t], o_recv.at[t], partner).wait_recv()
    for t, dst in enumerate((gk_hbm, gv_hbm)):
        for j in range(GROUPS):
            place = dst.at[:, cols(j, other)]
            remote(fin.at[g, j, :, pl.ds(t * HEAD, HEAD)], place, f_send.at[t, j], f_recv.at[t, j], partner).wait_recv()
    for copy in drains:
        copy.wait_send()


def attention(starts, queries, grad_out, keys, values):
    bf16 = jnp.bfloat16
    dma = pltpu.SemaphoreType.DMA
    any_space = pl.BlockSpec(memory_space=pl.ANY)
    wide = GROUPS * GROUP_HEADS * HEAD
    chunks = GROUPS // CHUNK
    return pl.pallas_call(
        kernel,
        out_shape=(
            jax.ShapeDtypeStruct(queries.shape, bf16),
            jax.ShapeDtypeStruct(queries.shape, bf16),
            jax.ShapeDtypeStruct(keys.shape, bf16),
            jax.ShapeDtypeStruct(keys.shape, bf16),
        ),
        in_specs=[pl.BlockSpec(memory_space=pltpu.VMEM)] + [any_space] * 4,
        out_specs=(any_space,) * 4,
        scratch_shapes=[
            pltpu.VMEM((GROUPS, SLOTS * RING * ROWS, KV), bf16),
            pltpu.VMEM((2, 2, ROWS, wide), bf16),
            pltpu.VMEM((2, 2, ROWS, wide), bf16),
            pltpu.VMEM((GROUPS, SLOTS * RING * ROWS, KV), jnp.float32),
            pltpu.VMEM((GROUPS, 2, HOPS, SLOTS, ROWS, KV), bf16),
            pltpu.VMEM((GROUPS, 2, HOPS, SLOTS, ROWS, KV), bf16),
            pltpu.VMEM((GROUPS, 3, RING, ROWS, KV), bf16),
            pltpu.VMEM((GROUPS, 3, RING, ROWS, KV), bf16),
            pltpu.VMEM((2, GROUPS, ROWS, KV), bf16),
            dma((2, GROUPS)), dma((2, GROUPS)), dma((2, GROUPS)),
            dma((2,)), dma((2,)), dma((2,)),
            dma((chunks, 3, RING)), dma((chunks, 3, RING)),
            dma((chunks, SLOTS, 2, HOPS)), dma((chunks, SLOTS, 2, HOPS)),
            dma((GROUPS, 2, HOPS, SLOTS)), dma((GROUPS, 2, HOPS, SLOTS)),
            dma((GROUPS, 3, RING)), dma((GROUPS, 3, RING)),
            dma((2,)), dma((2,)), dma((2,)),
            dma((2, GROUPS)), dma((2, GROUPS)), dma((2, GROUPS)),
        ],
        compiler_params=pltpu.CompilerParams(
            collective_id=0, has_side_effects=True, vmem_limit_bytes=58 * 1024 * 1024
        ),
    )(starts, queries, grad_out, keys, values)


def window_starts(doc_ids, first):
    ids = lax.dynamic_slice_in_dim(doc_ids, first, ROWS)
    begin = jnp.sum((doc_ids[None, :] < ids[:, None]).astype(jnp.int32), axis=1)
    rel = begin - (first - (WIN - ROWS))
    return jnp.tile(rel, 128 // ROWS)[None, :]


def local(queries, keys, values, doc_ids, grad_out):
    first = lax.axis_index("ctx") // 2 * (2 * RING * ROWS) + lax.axis_index("head") * ROWS
    starts = jnp.stack([window_starts(doc_ids, first), window_starts(doc_ids, first + RING * ROWS)])
    return attention(starts, queries, grad_out, keys, values)


def solution(mesh):
    spec = P(("ctx", "head"), None)
    return jax.shard_map(
        local,
        mesh=mesh,
        in_specs=(spec, spec, spec, P(), spec),
        out_specs=(spec, spec, spec, spec),
        check_vma=False,
    )
```

time: 100 us -> 87.4 us (0.87)
  Pallas kernels: 92.6 us -> 79.6 us
    pallas_call x1, Pallas kernels: 92.6 us -> 79.6 us  [attention(): pl.pallas_call(kernel, out_shape=(jax.ShapeDtypeStruct(queries.shape, bf1...]
where the time goes in v2:
time: 87.4 us; the launch traced here: 87.1 us
  Pallas kernels  79.6 us (91%)
  local copies, waits for them, and re-layouts  5.79 us (7%)
  other arithmetic  0.99 us (1%)
    pallas_call x1, Pallas kernels, attention(): pl.pallas_call(kernel, out_shape=(jax.ShapeDtypeStruct(queries.shape, bf1...  79.6 us
    unnamed x12, local copies, waits for them, and re-layouts  5.55 us

profile of v2, /device:TPU:1, one launch (start us, length us, event | category | flops | bytes accessed | tf_op | source)
XLA Modules:
  0.0 87.1 jit_solution(3011372846292251623)
XLA Ops:
  0.6 0.0 copy-start.3
  0.7 0.7 copy-done.3
  1.4 0.1 fusion
  1.5 0.4 convert_reduce_fusion.1
  1.9 0.1 stack_broadcast_in_dim_tile.7
  2.0 0.1 stack_broadcast_in_dim_tile.6
  2.1 0.6 pad_add_fusion.start_ref
  2.6 79.6 %shard_map.84 = (bf16[32,16384]{1,0:T(8,128)(2,1)}, bf16[32,16384]{1,0:T(8,128)(2,1)}, bf16[32,1024]{1,0:T(8,128)(2,1)}, bf16[32,1024]{1,0:T(8,128)(2,1)}) custom-call(s32[2,1,128]{2,1,0:T(1,128)} %pad_add_fusion.start_ref, bf16[32,16384]{1,0:T(8,128)(2,1)} %q_hbm.1, bf16[32,16384]{1,0:T(8,128)(2,1)} %do_hbm.1, bf16[32,1024]{1,0:T(8,128)(2,1)} %k_hbm.1, ...), custom_call_target="tpu_custom_call" | custom-call | tf_op jit(solution)/shard_map/pallas_call | solution.py:397
  82.3 0.0 copy-start
  82.3 2.4 %copy.13 = bf16[32,16384]{1,0:T(8,128)(2,1)} copy(bf16[32,16384]{1,0:T(8,128)(2,1)} %get-tuple-element.14) | data formatting | bytes 2097152
  84.7 0.0 copy-done
  84.7 0.0 copy-start.2
  84.7 1.0 %copy.14 = bf16[32,16384]{1,0:T(8,128)(2,1)} copy(bf16[32,16384]{1,0:T(8,128)(2,1)S(1)} %copy-done) | data formatting | bytes 2097152
  85.6 0.0 copy-done.2
  85.6 0.0 copy-start.1
  85.6 0.6 copy.15
  86.3 0.2 copy-done.1
  86.5 0.6 copy.16
  (3 shorter events, 0.0 us)
Async XLA Ops:
  0.6 0.8 copy-start.3
  82.3 2.4 %copy-start = (bf16[32,16384]{1,0:T(8,128)(2,1)S(1)}, bf16[32,16384]{1,0:T(8,128)(2,1)}, u32[]{:S(2)}) copy-start(bf16[32,16384]{1,0:T(8,128)(2,1)} %get-tuple-element.15) | copy-start | bytes 3145732
  84.7 1.0 %copy-start.2 = (bf16[32,1024]{1,0:T(8,128)(2,1)S(1)}, bf16[32,1024]{1,0:T(8,128)(2,1)}, u32[]{:S(2)}) copy-start(bf16[32,1024]{1,0:T(8,128)(2,1)} %get-tuple-element.16) | copy-start | bytes 196612
  85.6 0.9 copy-start.1
